TPU v7x, 256 devices: a whole 4x4x8 slice. The times are simulated.
256 devices in a mesh: task: 8 (over x, core), fsdp: 32 (over z, y).
Axes of the slice: x: 4, y: 4, z: 8, core: 2. Of those that a mesh axis runs over, the one named last changes fastest.
Arguments:
- grads_first: bfloat16 [16, 4096, 4096], P('task', 'fsdp'), may hold values from -120 to 120
- weights_first: float32 [4096, 4096], P('fsdp', 'task'), may hold values from -6 to 6
- moment_first: float32 [4096, 4096], P('fsdp', 'task'), may hold values from -3 to 3
- variance_first: float32 [4096, 4096], P('fsdp', 'task'), may hold values from 0.0025 to 1
- grads_second: bfloat16 [16, 4096, 4096], P('task', 'fsdp'), may hold values from -120 to 120
- weights_second: float32 [4096, 4096], P('fsdp', 'task'), may hold values from -6 to 6
- moment_second: float32 [4096, 4096], P('fsdp', 'task'), may hold values from -3 to 3
- variance_second: float32 [4096, 4096], P('fsdp', 'task'), may hold values from 0.0025 to 1
Outputs:
- combined_first: float32 [4096, 4096], P('fsdp', 'task')
- new_weights_first: float32 [4096, 4096], P('fsdp', 'task')
- new_moment_first: float32 [4096, 4096], P('fsdp', 'task')
- new_variance_first: float32 [4096, 4096], P('fsdp', 'task')
- combined_second: float32 [4096, 4096], P('fsdp', 'task')
- new_weights_second: float32 [4096, 4096], P('fsdp', 'task')
- new_moment_second: float32 [4096, 4096], P('fsdp', 'task')
- new_variance_second: float32 [4096, 4096], P('fsdp', 'task')
All inputs are finite; a program needn't handle non-finite values.
Results may differ from a plain program's by a relative error of at most 0.0006.
Values may be sent and summed in bfloat16 or wider, within the bound.
A program may use at most 128 MiB of HBM per device.

v0:
```python
import jax
import jax.numpy as jnp
from jax import lax
from jax.sharding import PartitionSpec as P

ITERS = 20
temper = 0.05
beta_one = 0.9
beta_two = 0.999
learn_rate = 0.001
adam_step = 1000.0
epsilon = 1e-08


def frank_wolfe(gram):
    scaled = gram / jnp.max(jnp.diagonal(gram))

    def advance(iteration, mixture):
        slope = 2.0 * jnp.dot(scaled, mixture, precision=lax.Precision.HIGHEST)
        expweights = jnp.exp(-slope / temper)
        vertex = expweights / jnp.sum(expweights)
        stepsize = 2.0 / (jnp.asarray(iteration).astype(jnp.float32) + 2.0)
        return mixture + stepsize * (vertex - mixture)

    start_mix = jnp.full((gram.shape[0],), 1.0 / gram.shape[0], jnp.float32)
    return lax.fori_loop(0, ITERS, advance, start_mix)


def adam_update(weights, moment, variance, combined):
    new_moment = beta_one * moment + (1.0 - beta_one) * combined
    new_variance = beta_two * variance + (1.0 - beta_two) * combined * combined
    corrected = new_moment / (1.0 - beta_one**adam_step)
    scaled_var = new_variance / (1.0 - beta_two**adam_step)
    new_weights = weights - learn_rate * corrected / (jnp.sqrt(scaled_var) + epsilon)
    return (new_weights, new_moment, new_variance)


def weighted_sum(mixture, stacked):
    return jnp.sum(mixture[:, None, None] * stacked.astype(jnp.float32), axis=0)


def prepare_first(gradients):
    regrouped = lax.all_to_all(gradients, "task", split_axis=2, concat_axis=0, tiled=True)
    return (
        regrouped,
        jnp.einsum("tre,sre->ts", regrouped, regrouped, preferred_element_type=jnp.float32),
    )


def prepare_second(gradients):
    regrouped = lax.all_to_all(gradients, "task", split_axis=2, concat_axis=0, tiled=True)
    return (
        regrouped,
        jnp.einsum("tre,sre->ts", regrouped, regrouped, preferred_element_type=jnp.float32),
    )


def combine_first(retained, mixture):
    return weighted_sum(mixture, retained)


def combine_second(retained, mixture):
    return weighted_sum(mixture, retained)


def local(
    grads_first,
    weights_first,
    moment_first,
    variance_first,
    grads_second,
    weights_second,
    moment_second,
    variance_second,
):
    retained_first, partial_first = prepare_first(grads_first)
    retained_second, partial_second = prepare_second(grads_second)
    gram_first, gram_second = lax.psum((partial_first, partial_second), ("task", "fsdp"))
    mixture_first = frank_wolfe(gram_first)
    mixture_second = frank_wolfe(gram_second)
    combined_first = combine_first(retained_first, mixture_first)
    first_w, first_m, first_v = adam_update(
        weights_first, moment_first, variance_first, combined_first
    )
    combined_second = combine_second(retained_second, mixture_second)
    second_w, second_m, second_v = adam_update(
        weights_second, moment_second, variance_second, combined_second
    )
    return (
        combined_first,
        first_w,
        first_m,
        first_v,
        combined_second,
        second_w,
        second_m,
        second_v,
    )


def solution(mesh):
    in_specs = (
        P("task", "fsdp", None),
        P("fsdp", "task"),
        P("fsdp", "task"),
        P("fsdp", "task"),
        P("task", "fsdp", None),
        P("fsdp", "task"),
        P("fsdp", "task"),
        P("fsdp", "task"),
    )
    out_specs = (
        P("fsdp", "task"),
        P("fsdp", "task"),
        P("fsdp", "task"),
        P("fsdp", "task"),
        P("fsdp", "task"),
        P("fsdp", "task"),
        P("fsdp", "task"),
        P("fsdp", "task"),
    )
    return jax.shard_map(local, mesh=mesh, in_specs=in_specs, out_specs=out_specs, check_vma=False)
```

profile of v0, /device:TPU:1, one launch (start us, length us, event | category | flops | bytes accessed | tf_op | source)
XLA Modules:
  0.0 235.0 jit_solution(9579224308458622726)
XLA Ops:
  0.6 6.2 %copy.25 = bf16[2,128,4096]{1,0,2:T(2,128)(2,1)} copy(bf16[2,128,4096]{2,1,0:T(8,128)(2,1)} %param.16) | data formatting | bytes 4194304 | tf_op args[4]
  6.8 6.7 %all-to-all-start.1 = ((bf16[2,128,4096]{1,0,2:T(2,128)(2,1)}), bf16[2,128,4096]{1,0,2:T(2,128)(2,1)S(1)}, u32[]{:S(2)}, u32[]{:S(2)}) async-start(bf16[2,128,4096]{1,0,2:T(2,128)(2,1)} %copy.25), calls=%async_computation.1 | async-start | bytes 4194304 | tf_op jit(solution)/shard_map/all_to_all | solution.py:51
  13.6 6.2 %copy.20 = bf16[2,128,4096]{1,0,2:T(2,128)(2,1)} copy(bf16[2,128,4096]{2,1,0:T(8,128)(2,1)} %param.12) | data formatting | bytes 4194304 | tf_op args[0]
  19.7 20.2 %all-to-all-done.1 = bf16[2,128,4096]{1,0,2:T(2,128)(2,1)S(1)} async-done(((bf16[2,128,4096]{1,0,2:T(2,128)(2,1)}), bf16[2,128,4096]{1,0,2:T(2,128)(2,1)S(1)}, u32[]{:S(2)}, u32[]{:S(2)}) %all-to-all-start.1) | async-done | bytes 2097184 | tf_op jit(solution)/shard_map/all_to_all | solution.py:51
  39.9 1.3 copy-done
  41.2 4.4 %all-to-all-start = ((bf16[2,128,4096]{1,0,2:T(2,128)(2,1)}), bf16[2,128,4096]{1,0,2:T(2,128)(2,1)S(1)}, u32[]{:S(2)}, u32[]{:S(2)}) async-start(bf16[2,128,4096]{1,0,2:T(2,128)(2,1)} %copy.20), calls=%async_computation | async-start | bytes 4194304 | tf_op jit(solution)/shard_map/all_to_all | solution.py:43
  45.8 0.8 copy.28
  46.6 0.8 copy.29
  47.6 1.1 copy.23
  48.8 3.0 %copy.26 = bf16[2,128,8,512]{1,0,2,3:T(2,128)(2,1)S(1)} copy(bf16[2,128,8,512]{1,0,3,2:T(2,128)(2,1)} %bitcast.62) | data formatting | bytes 4194304 | tf_op jit(solution)/shard_map/all_to_all | solution.py:51
  51.8 0.9 convolution_bitcast_fusion.2
  52.7 19.2 %all-to-all-done = bf16[2,128,4096]{1,0,2:T(2,128)(2,1)S(1)} async-done(((bf16[2,128,4096]{1,0,2:T(2,128)(2,1)}), bf16[2,128,4096]{1,0,2:T(2,128)(2,1)S(1)}, u32[]{:S(2)}, u32[]{:S(2)}) %all-to-all-start) | async-done | bytes 2097184 | tf_op jit(solution)/shard_map/all_to_all | solution.py:43
  72.0 1.4 copy.21
  73.4 0.9 convolution_bitcast_fusion.3
  74.3 78.4 %all-reduce = (f32[16,16]{1,0:T(8,128)S(1)}, f32[16,16]{1,0:T(8,128)S(1)}) all-reduce(f32[16,16]{1,0:T(8,128)S(1)} %convolution_bitcast_fusion.3, f32[16,16]{1,0:T(8,128)S(1)} %convolution_bitcast_fusion.2), channel_id=1, replica_groups=mesh['task'=8,'fsdp'=32] {'task','fsdp'}, use_global_device_ids=true, to_apply=%region_0.0 | all-reduce | flops 512 | bytes 4096 | tf_op jit(solution)/shard_map/psum | solution.py:78
  155.2 1.3 broadcast_divide_fusion
  156.5 29.4 %while.29 = (s32[]{:T(128)}, f32[16]{0:T(128)S(1)}, f32[16,16]{1,0:T(8,128)S(1)}, s32[]{:T(128)}, s32[]{:T(128)}, /*index=5*/f32[]{:T(128)}) while((s32[]{:T(128)}, f32[16]{0:T(128)S(1)}, f32[16,16]{1,0:T(8,128)S(1)}, s32[]{:T(128)}, s32[]{:T(128)}, /*index=5*/f32[]{:T(128)}) %tuple.78), condition=%wide.region_10.11_spmd.clone, body=%wide.region_8.10_spmd.clone.sunk | while | flops 3237 | bytes 1468 | solution.py:26
  156.6 0.7 fusion.31
  158.0 0.7 fusion.31
  159.5 0.7 fusion.31
  162.4 0.7 fusion.31
  163.9 0.7 fusion.31
  165.4 0.7 fusion.31
  168.3 0.7 fusion.31
  169.8 0.7 fusion.31
  171.3 0.7 fusion.31
  174.2 0.7 fusion.31
  175.7 0.7 fusion.31
  177.2 0.7 fusion.31
  178.6 0.7 fusion.31
  180.1 0.7 fusion.31
  181.6 0.7 fusion.31
  183.1 0.7 fusion.31
  184.5 0.7 fusion.31
  186.1 4.7 %multiply_reduce_fusion = f32[128,512]{0,1:T(8,128)S(1)} fusion(f32[8,2]{1,0:T(8,128)S(1)} %mul.109, bf16[2,128,8,512]{1,0,3,2:T(2,128)(2,1)} %bitcast.63), kind=kLoop, calls=%fused_computation.22 | loop fusion | flops 3080192 | bytes 2359360 | tf_op jit(solution)/shard_map/reduce_sum | solution.py:39
  190.7 0.8 copy.34
  191.6 2.0 divide_subtract_fusion.2
  193.6 1.8 copy.35
  195.4 1.8 copy.36
  197.1 1.8 copy.37
  198.9 29.4 %while.28 = (s32[]{:T(128)}, f32[16]{0:T(128)S(1)}, f32[16,16]{1,0:T(8,128)S(1)}, s32[]{:T(128)}, s32[]{:T(128)}, /*index=5*/f32[]{:T(128)}) while((s32[]{:T(128)}, f32[16]{0:T(128)S(1)}, f32[16,16]{1,0:T(8,128)S(1)}, s32[]{:T(128)}, s32[]{:T(128)}, /*index=5*/f32[]{:T(128)}) %tuple.75), condition=%wide.region_4.0_spmd.clone, body=%wide.region_2.0_spmd.clone.sunk | while | flops 3237 | bytes 1468 | solution.py:26
  200.4 0.7 fusion.29
  201.9 0.7 fusion.29
  228.4 3.1 %multiply_reduce_fusion.1 = f32[128,512]{0,1:T(8,128)S(1)} fusion(f32[8,2]{1,0:T(8,128)S(1)} %mul.100, bf16[2,128,8,512]{1,0,3,2:T(2,128)(2,1)S(1)} %bitcast.61), kind=kLoop, calls=%fused_computation.23 | loop fusion | flops 3080192 | bytes 2359360 | tf_op jit(solution)/shard_map/reduce_sum | solution.py:39
  231.5 0.8 copy.30
  232.5 0.8 copy.31
  233.4 0.8 copy.32
  234.2 0.8 copy.33
  (85 shorter events, 45.4 us)
Async XLA Ops:
  6.8 33.1 %all-to-all-start.1 = ((bf16[2,128,4096]{1,0,2:T(2,128)(2,1)}), bf16[2,128,4096]{1,0,2:T(2,128)(2,1)S(1)}, u32[]{:S(2)}, u32[]{:S(2)}) async-start(bf16[2,128,4096]{1,0,2:T(2,128)(2,1)} %copy.25), calls=%async_computation.1 | async-start | bytes 4194304 | tf_op jit(solution)/shard_map/all_to_all | solution.py:51
  19.7 25.9 %copy-start.1 = (f32[128,512]{1,0:T(8,128)S(1)}, f32[128,512]{1,0:T(8,128)}, u32[]{:S(2)}) copy-start(f32[128,512]{1,0:T(8,128)} %param.18) | copy-start | bytes 786436
  19.7 26.0 %copy-start.2 = (f32[128,512]{1,0:T(8,128)S(1)}, f32[128,512]{1,0:T(8,128)}, u32[]{:S(2)}) copy-start(f32[128,512]{1,0:T(8,128)} %param.19) | copy-start | bytes 786436
  19.7 26.9 %copy-start.3 = (f32[128,512]{1,0:T(8,128)S(1)}, f32[128,512]{1,0:T(8,128)}, u32[]{:S(2)}) copy-start(f32[128,512]{1,0:T(8,128)} %param.17) | copy-start | bytes 786436
  19.7 27.7 %copy-start.4 = (f32[128,512]{1,0:T(8,128)S(1)}, f32[128,512]{1,0:T(8,128)}, u32[]{:S(2)}) copy-start(f32[128,512]{1,0:T(8,128)} %param.14) | copy-start | bytes 786436
  39.9 1.3 copy-start
  41.2 30.7 %all-to-all-start = ((bf16[2,128,4096]{1,0,2:T(2,128)(2,1)}), bf16[2,128,4096]{1,0,2:T(2,128)(2,1)S(1)}, u32[]{:S(2)}, u32[]{:S(2)}) async-start(bf16[2,128,4096]{1,0,2:T(2,128)(2,1)} %copy.20), calls=%async_computation | async-start | bytes 4194304 | tf_op jit(solution)/shard_map/all_to_all | solution.py:43
  45.7 2.9 %copy-start.5 = (f32[128,512]{1,0:T(8,128)S(1)}, f32[128,512]{1,0:T(8,128)}, u32[]{:S(2)}) copy-start(f32[128,512]{1,0:T(8,128)} %param.13) | copy-start | bytes 786436
where the time goes:
time: 236 us; the launch traced here: 235 us
  blocking collectives  78.4 us (33%)
  waiting for transfers between devices  39.4 us (17%)
  other arithmetic  38.9 us (16%)
  local copies, waits for them, and re-layouts  32.3 us (14%)
  matrix products  31.6 us (13%)
  starting transfers between devices  11.1 us (5%)
  loops' own time  2.61 us (1%)
    psum x1, blocking collectives, local(): lax.psum((partial_first, partial_second), ('task', 'fsdp'))  78.4 us
    dot_general x40, matrix products, advance(): slope = 2.0 * jnp.dot(scaled, mixture, precision=lax.Precision.HIGHEST)  29.8 us
    add x40, other arithmetic, advance(): return mixture + stepsize * (vertex - mixture)  26.5 us
    unnamed x28, local copies, waits for them, and re-layouts  26.3 us
    all_to_all x1, waiting for transfers between devices, prepare_second(): lax.all_to_all(gradients, 'task', split_axis=2, concat_axis=0, tiled=True)  20.2 us
    all_to_all x1, waiting for transfers between devices, prepare_first(): lax.all_to_all(gradients, 'task', split_axis=2, concat_axis=0, tiled=True)  19.2 us
    reduce_sum x2, other arithmetic, weighted_sum(): return jnp.sum(mixture[:, None, None] * stacked.astype(jnp.float32), axis=0)  7.72 us
    all_to_all x1, starting transfers between devices, prepare_second(): lax.all_to_all(gradients, 'task', split_axis=2, concat_axis=0, tiled=True)  6.74 us
  transfers between devices with their start and end apart: 2, of which 2 were waited for; matrix products, arithmetic and copies ran while one was open for 6% of the time, Pallas kernels for 0%

commit v1 on v0

--- a/solution.py
+++ b/solution.py
@@ -75,7 +75,7 @@
 ):
     retained_first, partial_first = prepare_first(grads_first)
     retained_second, partial_second = prepare_second(grads_second)
-    gram_first, gram_second = lax.psum((partial_first, partial_second), ("task", "fsdp"))
+    gram_first, gram_second = lax.psum(lax.psum((partial_first, partial_second), "task"), "fsdp")
     mixture_first = frank_wolfe(gram_first)
     mixture_second = frank_wolfe(gram_second)
     combined_first = combine_first(retained_first, mixture_first)

time: 236 us -> 324 us (1.37)
  the two profiles are of different devices: /device:TPU:1 before, /device:TPU:0 now
where the time goes in v1:
time: 324 us; the launch traced here: 323 us
  blocking collectives  169 us (52%)
  waiting for transfers between devices  40.9 us (13%)
  other arithmetic  38.9 us (12%)
  local copies, waits for them, and re-layouts  32.3 us (10%)
  matrix products  31.6 us (10%)
  starting transfers between devices  7.2 us (2%)
    psum x1, blocking collectives, local(): lax.psum(lax.psum((partial_first, partial_second), 'task'), 'fsdp')  145 us
    dot_general x40, matrix products, advance(): slope = 2.0 * jnp.dot(scaled, mixture, precision=lax.Precision.HIGHEST)  29.8 us
    add x40, other arithmetic, advance(): return mixture + stepsize * (vertex - mixture)  26.5 us
    unnamed x28, local copies, waits for them, and re-layouts  26.3 us
    psum x1, blocking collectives, local(): lax.psum((partial_first, partial_second), 'task')  23.8 us
    all_to_all x1, waiting for transfers between devices, prepare_second(): lax.all_to_all(gradients, 'task', split_axis=2, concat_axis=0, tiled=True)  20.9 us
    all_to_all x1, waiting for transfers between devices, prepare_first(): lax.all_to_all(gradients, 'task', split_axis=2, concat_axis=0, tiled=True)  20 us
    reduce_sum x2, other arithmetic, weighted_sum(): return jnp.sum(mixture[:, None, None] * stacked.astype(jnp.float32), axis=0)  7.72 us
  transfers between devices with their start and end apart: 2, of which 2 were waited for; matrix products, arithmetic and copies ran while one was open for 4% of the time, Pallas kernels for 0%

profile of v1, /device:TPU:0, one launch (start us, length us, event | category | flops | bytes accessed | tf_op | source)
XLA Modules:
  0.0 323.3 jit_solution(11171397481924810321)
XLA Ops:
  0.6 6.2 %copy.25 = bf16[2,128,4096]{1,0,2:T(2,128)(2,1)} copy(bf16[2,128,4096]{2,1,0:T(8,128)(2,1)} %param.16) | data formatting | bytes 4194304 | tf_op args[4]
  6.8 3.6 %all-to-all-start.1 = ((bf16[2,128,4096]{1,0,2:T(2,128)(2,1)}), bf16[2,128,4096]{1,0,2:T(2,128)(2,1)S(1)}, u32[]{:S(2)}, u32[]{:S(2)}) async-start(bf16[2,128,4096]{1,0,2:T(2,128)(2,1)} %copy.25), calls=%async_computation.1 | async-start | bytes 4194304 | tf_op jit(solution)/shard_map/all_to_all | solution.py:51
  10.4 6.2 %copy.20 = bf16[2,128,4096]{1,0,2:T(2,128)(2,1)} copy(bf16[2,128,4096]{2,1,0:T(8,128)(2,1)} %param.12) | data formatting | bytes 4194304 | tf_op args[0]
  16.6 20.9 %all-to-all-done.1 = bf16[2,128,4096]{1,0,2:T(2,128)(2,1)S(1)} async-done(((bf16[2,128,4096]{1,0,2:T(2,128)(2,1)}), bf16[2,128,4096]{1,0,2:T(2,128)(2,1)S(1)}, u32[]{:S(2)}, u32[]{:S(2)}) %all-to-all-start.1) | async-done | bytes 2097184 | tf_op jit(solution)/shard_map/all_to_all | solution.py:51
  37.6 1.3 copy-done
  38.9 3.6 %all-to-all-start = ((bf16[2,128,4096]{1,0,2:T(2,128)(2,1)}), bf16[2,128,4096]{1,0,2:T(2,128)(2,1)S(1)}, u32[]{:S(2)}, u32[]{:S(2)}) async-start(bf16[2,128,4096]{1,0,2:T(2,128)(2,1)} %copy.20), calls=%async_computation | async-start | bytes 4194304 | tf_op jit(solution)/shard_map/all_to_all | solution.py:43
  42.6 0.8 copy.28
  43.5 0.8 copy.29
  44.5 1.1 copy.23
  45.7 3.0 copy.26
  48.7 0.9 convolution_bitcast_fusion.2
  49.6 20.0 %all-to-all-done = bf16[2,128,4096]{1,0,2:T(2,128)(2,1)S(1)} async-done(((bf16[2,128,4096]{1,0,2:T(2,128)(2,1)}), bf16[2,128,4096]{1,0,2:T(2,128)(2,1)S(1)}, u32[]{:S(2)}, u32[]{:S(2)}) %all-to-all-start) | async-done | bytes 2097184 | tf_op jit(solution)/shard_map/all_to_all | solution.py:43
  69.6 1.4 copy.21
  71.0 0.9 convolution_bitcast_fusion.3
  71.9 23.8 %all-reduce.1 = (f32[16,16]{1,0:T(8,128)S(1)}, f32[16,16]{1,0:T(8,128)S(1)}) all-reduce(f32[16,16]{1,0:T(8,128)S(1)} %convolution_bitcast_fusion.3, f32[16,16]{1,0:T(8,128)S(1)} %convolution_bitcast_fusion.2), channel_id=1, replica_groups=mesh['task'=8,'fsdp'=32] {'task'}, use_global_device_ids=true, to_apply=%region_0.0 | all-reduce | flops 512 | bytes 4096 | tf_op jit(solution)/shard_map/psum | solution.py:78
  95.8 145.2 %all-reduce = (f32[16,16]{1,0:T(8,128)S(1)}, f32[16,16]{1,0:T(8,128)S(1)}) all-reduce(f32[16,16]{1,0:T(8,128)S(1)} %get-tuple-element.184, f32[16,16]{1,0:T(8,128)S(1)} %get-tuple-element.185), channel_id=1, replica_groups=mesh['task'=8,'fsdp'=32] {'fsdp'}, use_global_device_ids=true, to_apply=%region_1.0 | all-reduce | flops 512 | bytes 4096 | tf_op jit(solution)/shard_map/psum | solution.py:78
  243.5 1.3 broadcast_divide_fusion
  244.8 29.4 %while.29 = (s32[]{:T(128)}, f32[16]{0:T(128)S(1)}, f32[16,16]{1,0:T(8,128)S(1)}, s32[]{:T(128)}, s32[]{:T(128)}, /*index=5*/f32[]{:T(128)}) while((s32[]{:T(128)}, f32[16]{0:T(128)S(1)}, f32[16,16]{1,0:T(8,128)S(1)}, s32[]{:T(128)}, s32[]{:T(128)}, /*index=5*/f32[]{:T(128)}) %tuple.78), condition=%wide.region_12.13_spmd.clone, body=%wide.region_10.12_spmd.clone.sunk | while | flops 3237 | bytes 1468 | solution.py:26
  246.3 0.7 fusion.31
  247.8 0.7 fusion.31
  249.2 0.7 fusion.31
  250.7 0.7 fusion.31
  252.2 0.7 fusion.31
  253.7 0.7 fusion.31
  255.1 0.7 fusion.31
  256.6 0.7 fusion.31
  258.1 0.7 fusion.31
  259.5 0.7 fusion.31
  262.5 0.7 fusion.31
  264.0 0.7 fusion.31
  265.4 0.7 fusion.31
  268.4 0.7 fusion.31
  269.8 0.7 fusion.31
  271.3 0.7 fusion.31
  274.3 4.7 %multiply_reduce_fusion = f32[128,512]{0,1:T(8,128)S(1)} fusion(f32[8,2]{1,0:T(8,128)S(1)} %mul.109, bf16[2,128,8,512]{1,0,3,2:T(2,128)(2,1)} %bitcast.63), kind=kLoop, calls=%fused_computation.22 | loop fusion | flops 3080192 | bytes 2359360 | tf_op jit(solution)/shard_map/reduce_sum | solution.py:39
  279.0 0.8 copy.34
  279.8 2.0 divide_subtract_fusion.2
  281.8 1.8 copy.35
  283.6 1.8 copy.36
  285.4 1.8 copy.37
  287.2 29.4 %while.28 = (s32[]{:T(128)}, f32[16]{0:T(128)S(1)}, f32[16,16]{1,0:T(8,128)S(1)}, s32[]{:T(128)}, s32[]{:T(128)}, /*index=5*/f32[]{:T(128)}) while((s32[]{:T(128)}, f32[16]{0:T(128)S(1)}, f32[16,16]{1,0:T(8,128)S(1)}, s32[]{:T(128)}, s32[]{:T(128)}, /*index=5*/f32[]{:T(128)}) %tuple.75), condition=%wide.region_5.6_spmd.clone, body=%wide.region_3.5_spmd.clone.sunk | while | flops 3237 | bytes 1468 | solution.py:26
  290.1 0.7 fusion.29
  291.6 0.7 fusion.29
  316.7 3.1 multiply_reduce_fusion.1
  319.8 0.8 copy.30
  320.8 0.8 copy.31
  321.6 0.8 copy.32
  322.5 0.8 copy.33
  (86 shorter events, 46.1 us)
Async XLA Ops:
  6.8 30.7 %all-to-all-start.1 = ((bf16[2,128,4096]{1,0,2:T(2,128)(2,1)}), bf16[2,128,4096]{1,0,2:T(2,128)(2,1)S(1)}, u32[]{:S(2)}, u32[]{:S(2)}) async-start(bf16[2,128,4096]{1,0,2:T(2,128)(2,1)} %copy.25), calls=%async_computation.1 | async-start | bytes 4194304 | tf_op jit(solution)/shard_map/all_to_all | solution.py:51
  16.6 25.9 %copy-start.1 = (f32[128,512]{1,0:T(8,128)S(1)}, f32[128,512]{1,0:T(8,128)}, u32[]{:S(2)}) copy-start(f32[128,512]{1,0:T(8,128)} %param.18) | copy-start | bytes 786436
  16.6 26.0 %copy-start.2 = (f32[128,512]{1,0:T(8,128)S(1)}, f32[128,512]{1,0:T(8,128)}, u32[]{:S(2)}) copy-start(f32[128,512]{1,0:T(8,128)} %param.19) | copy-start | bytes 786436
  16.6 26.9 %copy-start.3 = (f32[128,512]{1,0:T(8,128)S(1)}, f32[128,512]{1,0:T(8,128)}, u32[]{:S(2)}) copy-start(f32[128,512]{1,0:T(8,128)} %param.17) | copy-start | bytes 786436
  16.6 27.7 %copy-start.4 = (f32[128,512]{1,0:T(8,128)S(1)}, f32[128,512]{1,0:T(8,128)}, u32[]{:S(2)}) copy-start(f32[128,512]{1,0:T(8,128)} %param.14) | copy-start | bytes 786436
  37.6 1.3 copy-start
  38.9 30.7 %all-to-all-start = ((bf16[2,128,4096]{1,0,2:T(2,128)(2,1)}), bf16[2,128,4096]{1,0,2:T(2,128)(2,1)S(1)}, u32[]{:S(2)}, u32[]{:S(2)}) async-start(bf16[2,128,4096]{1,0,2:T(2,128)(2,1)} %copy.20), calls=%async_computation | async-start | bytes 4194304 | tf_op jit(solution)/shard_map/all_to_all | solution.py:43
  42.6 2.9 copy-start.5
